TPU v7x, 256 devices: a whole 4x4x8 slice. The times are simulated.
256 devices in a mesh: slab: 16 (over x, z_lo, core), kern: 16 (over z_hi, y).
Axes of the slice: x: 4, y: 4, z: 8 (z_hi: 4, z_lo: 2; z = z_hi * 2 + z_lo), core: 2. Of those that a mesh axis runs over, the one named last changes fastest.
Arguments:
- mask_level: float32 [1024, 1024], P('slab'), may hold values from 0 to 1
- kernel_spectra: float32 [16, 2, 1024, 1024], P('kern', None, 'slab'), may hold values from -4.2 to 4.2
- socs_weight: float32 [16], replicated, may hold values from 0.05 to 0.5
- kernel_slot: int32 [16], replicated, may hold values from 0 to 15, each once
- blur_taps: float32 [31], replicated, may hold values from 0.005 to 0.06
- target: int32 [1024, 1024], P('slab'), may hold values 0 or 1
Outputs:
- mask_gradient: float32 [1024, 1024], P('slab', 'kern')
- resist_image: float32 [1024, 1024], P('slab', 'kern')
Inputs may be any that keep to these rules, and one draw needn't show every extreme that they name: `target`: every cell is 0 or 1. `kernel_slot`: each kernel number stands at exactly one slot.
All inputs are finite; a program needn't handle non-finite values. No bound on the sum of `target` on one device may be relied on, other than what follows from the above.
Results may differ from a plain program's by a relative error of at most 0.00017.
Values sent between devices are 32-bit elements; how exact they have to be, the bound alone decides.
A program may use at most 64 MiB of HBM per device.

v0:
```python
import math
import jax
import jax.numpy as jnp
from jax import lax
from jax.sharding import PartitionSpec as P

CQ = 128
STEEP = 4.0
LEVEL = 0.5


def swapped(shard, axis, apart):
    return lax.ppermute(shard, axis, [(i, i ^ 1 << apart) for i in range(lax.axis_size(axis))])


def padded_2(shard, sides, width):
    for axis, dim in sides:
        devices, length = (lax.axis_size(axis), shard.shape[dim])
        up = [(i, (i + 1) % devices) for i in range(devices - 1)]
        down = [(j, i) for i, j in up]
        last = lax.slice_in_dim(shard, length - width, length, axis=dim)
        initial = lax.slice_in_dim(shard, 0, width, axis=dim)
        before = lax.ppermute(last, axis, up)
        after = lax.ppermute(initial, axis, down)
        shard = jnp.concatenate([before, shard, after], axis=dim)
    return shard


def reversed_bits(number, num_bits):
    result = number * 0
    for bit_pos in range(num_bits):
        result = result * 2 + number // 2**bit_pos % 2
    return result


def rotation(product, length, sign_val):
    fraction = (product % length).astype(jnp.float32) / length
    angles = sign_val * 2.0 * math.pi * fraction
    return (jnp.cos(angles), jnp.sin(angles))


def complex_mul(first_pair, second_pair):
    real_part = first_pair[0] * second_pair[0] - first_pair[1] * second_pair[1]
    imag_part = first_pair[0] * second_pair[1] + first_pair[1] * second_pair[0]
    return (real_part, imag_part)


def table_product(pattern, matrix, values):
    highest = lax.Precision.HIGHEST

    def single(first_op, second_op):
        return jnp.einsum(pattern, first_op, second_op, precision=highest)

    if values[1] is None:
        return (single(matrix[0], values[0]), single(matrix[1], values[0]))
    real_part = single(matrix[0], values[0]) - single(matrix[1], values[1])
    imag_part = single(matrix[0], values[1]) + single(matrix[1], values[0])
    return (real_part, imag_part)


def columns_forward(values, outer_len, inner_len):
    extent = values[0].shape[0]
    shaped = tuple(
        (None if piece is None else piece.reshape(extent, outer_len, inner_len) for piece in values)
    )
    outer_idx = jnp.arange(outer_len)
    inner_idx = jnp.arange(inner_len)
    section = table_product(
        "ab,rbq->raq", rotation(outer_idx[:, None] * outer_idx[None, :], outer_len, -1.0), shaped
    )
    section = complex_mul(
        section, rotation(outer_idx[:, None] * inner_idx[None, :], outer_len * inner_len, -1.0)
    )
    return table_product(
        "bk,rpb->rpk", rotation(inner_idx[:, None] * inner_idx[None, :], inner_len, -1.0), section
    )


def columns_inverse(values, outer_len, inner_len, real_only):
    extent = values[0].shape[0]
    outer_idx = jnp.arange(outer_len)
    inner_idx = jnp.arange(inner_len)
    section = table_product(
        "bk,rpb->rpk", rotation(inner_idx[:, None] * inner_idx[None, :], inner_len, 1.0), values
    )
    section = complex_mul(
        section, rotation(outer_idx[:, None] * inner_idx[None, :], outer_len * inner_len, 1.0)
    )
    matrix = rotation(outer_idx[:, None] * outer_idx[None, :], outer_len, 1.0)
    if real_only:
        highest = lax.Precision.HIGHEST
        real_part = jnp.einsum("ab,rbq->raq", matrix[0], section[0], precision=highest)
        real_part = real_part - jnp.einsum("ab,rbq->raq", matrix[1], section[1], precision=highest)
        return real_part.reshape(extent, outer_len * inner_len)
    result = table_product("ab,rbq->raq", matrix, section)
    return (
        result[0].reshape(extent, outer_len * inner_len),
        result[1].reshape(extent, outer_len * inner_len),
    )


def rows_forward(values, freq_offset, full_width):
    extent = values[0].shape[0]
    positions = jnp.arange(extent)
    twiddle = rotation(positions * freq_offset, full_width, -1.0)
    values = complex_mul(values, (twiddle[0][:, None], twiddle[1][:, None]))
    return table_product(
        "sr,rc->sc", rotation(positions[:, None] * positions[None, :], extent, -1.0), values
    )


def rows_inverse(values, freq_offset, full_width):
    extent = values[0].shape[0]
    positions = jnp.arange(extent)
    values = table_product(
        "rs,sc->rc", rotation(positions[:, None] * positions[None, :], extent, 1.0), values
    )
    twiddle = rotation(positions * freq_offset, full_width, 1.0)
    return complex_mul(values, (twiddle[0][:, None], twiddle[1][:, None]))


def pairs_forward(stacked, num_bits):
    slab_index = lax.axis_index("slab")
    for bit_level in range(num_bits - 1, -1, -1):
        half_span = 2**bit_level
        partner = swapped(stacked, "slab", bit_level)
        is_upper = slab_index // half_span % 2 == 1
        twiddle = rotation(slab_index % half_span, 2 * half_span, -1.0)
        lower_val = stacked + partner
        difference = partner - stacked
        upper_val = jnp.stack(complex_mul((difference[0], difference[1]), twiddle))
        stacked = jnp.where(is_upper, upper_val, lower_val)
    return stacked


def pairs_inverse(stacked, num_bits):
    slab_index = lax.axis_index("slab")
    for bit_level in range(num_bits):
        half_span = 2**bit_level
        partner = swapped(stacked, "slab", bit_level)
        is_upper = slab_index // half_span % 2 == 1
        twiddle = rotation(slab_index % half_span, 2 * half_span, 1.0)
        from_upper = jnp.where(is_upper, stacked, partner)
        from_lower = jnp.where(is_upper, partner, stacked)
        turned = jnp.stack(complex_mul((from_upper[0], from_upper[1]), twiddle))
        stacked = jnp.where(is_upper, from_lower - turned, from_lower + turned)
    return stacked


def mix_forward(stacked, num_bits):
    return pairs_forward(stacked, num_bits)


def mix_inverse(stacked, num_bits):
    return pairs_inverse(stacked, num_bits)


def smooth(padded, kernel_taps, extent, span):
    tap_count = kernel_taps.shape[0]
    row_part = kernel_taps[0] * padded[0:extent, :]
    for tap_idx in range(1, tap_count):
        row_part = row_part + kernel_taps[tap_idx] * padded[tap_idx : tap_idx + extent, :]
    result = kernel_taps[0] * row_part[:, 0:span]
    for tap_idx in range(1, tap_count):
        result = result + kernel_taps[tap_idx] * row_part[:, tap_idx : tap_idx + span]
    return result


def resist_section(intensity_term, kernel_taps, target, kern_count, kern_index):
    reach = (kernel_taps.shape[0] - 1) // 2
    flipped = kernel_taps[::-1]
    extent, full_width = intensity_term.shape
    share_cols = full_width // kern_count

    def widen(values):
        padded = padded_2(values, (("slab", 0),), reach)
        return jnp.pad(padded, ((0, 0), (reach, reach)))

    summed = lax.psum(intensity_term, "kern")
    goal_cells = target.astype(jnp.float32)
    resist = jax.nn.sigmoid(
        STEEP * (smooth(widen(summed), kernel_taps, extent, full_width) - LEVEL)
    )
    slope_grad = 2.0 * (resist - goal_cells) * STEEP * resist * (1.0 - resist)
    cotangent = smooth(widen(slope_grad), flipped, extent, full_width)
    return (cotangent, lax.dynamic_slice_in_dim(resist, kern_index * share_cols, share_cols, 1))


def on_device(mask_level, kernel_spectra, socs_weight, kernel_slot, blur_taps, target):
    extent, full_width = mask_level.shape
    slab_count = lax.axis_size("slab")
    kern_count = lax.axis_size("kern")
    num_bits = slab_count.bit_length() - 1
    inner_len = CQ
    outer_len = full_width // inner_len
    freq_offset = reversed_bits(lax.axis_index("slab"), num_bits)
    kern_index = lax.axis_index("kern")
    kernel_id = jnp.sum(jnp.where(jnp.arange(kernel_slot.shape[0]) == kern_index, kernel_slot, 0))
    weight = jnp.sum(jnp.where(jnp.arange(socs_weight.shape[0]) == kernel_id, socs_weight, 0.0))
    arranged = kernel_spectra[0].reshape(2, extent, inner_len, outer_len).transpose(0, 1, 3, 2)
    transfer = (arranged[0], arranged[1])
    norm_scale = 1.0 / (full_width * full_width)

    def spectrum(values):
        columns = columns_forward(values, outer_len, inner_len)
        stacked = jnp.stack(columns).reshape(2, extent, full_width)
        stacked = mix_forward(stacked, num_bits)
        row_part = rows_forward((stacked[0], stacked[1]), freq_offset, full_width)
        return (
            row_part[0].reshape(extent, outer_len, inner_len),
            row_part[1].reshape(extent, outer_len, inner_len),
        )

    def back_to_cells(spectral, real_only):
        flat = (spectral[0].reshape(extent, full_width), spectral[1].reshape(extent, full_width))
        row_local = rows_inverse(flat, freq_offset, full_width)
        stacked = mix_inverse(jnp.stack(row_local), num_bits)
        shaped = (
            stacked[0].reshape(extent, outer_len, inner_len),
            stacked[1].reshape(extent, outer_len, inner_len),
        )
        return columns_inverse(shaped, outer_len, inner_len, real_only)

    mask_spec = spectrum((mask_level, None))
    field_val = back_to_cells(complex_mul(transfer, mask_spec), False)
    field_val = (field_val[0] * norm_scale, field_val[1] * norm_scale)
    intensity_term = weight * (field_val[0] * field_val[0] + field_val[1] * field_val[1])
    cotangent, resist = resist_section(intensity_term, blur_taps, target, kern_count, kern_index)
    factor = 2.0 * weight * cotangent
    carried_spec = spectrum((factor * field_val[0], factor * field_val[1]))
    gradient_term = (
        back_to_cells(complex_mul((transfer[0], -transfer[1]), carried_spec), True) * norm_scale
    )
    gradient = lax.psum_scatter(gradient_term, "kern", scatter_dimension=1, tiled=True)
    return (gradient, resist)


def solution(mesh):
    placed = (P("slab", None), P("kern", None, "slab", None), P(), P(), P(), P("slab", None))
    return jax.shard_map(
        on_device,
        mesh=mesh,
        in_specs=placed,
        out_specs=(P("slab", "kern"), P("slab", "kern")),
        check_vma=False,
    )
```

profile of v0, /device:TPU:2, one launch (start us, length us, event | category | flops | bytes accessed | tf_op | source)
XLA Modules:
  0.0 578.6 jit_solution(16228788483200270376)
XLA Ops:
  11.7 2.2 collective-permute-start
  14.1 12.9 %collective-permute-done = f32[2,64,1024]{2,1,0:T(8,128)S(1)} collective-permute-done((f32[2,64,1024]{2,1,0:T(8,128)S(1)}, f32[2,64,1024]{2,1,0:T(8,128)S(1)}, u32[]{:S(2)}, u32[]{:S(2)}) %collective-permute-start) | collective-permute-done | bytes 524320 | tf_op jit(solution)/shard_map/ppermute | solution.py:13
  27.8 12.3 %collective-permute-done.1 = f32[2,64,1024]{2,1,0:T(8,128)S(1)} collective-permute-done((f32[2,64,1024]{2,1,0:T(8,128)S(1)}, f32[2,64,1024]{2,1,0:T(8,128)S(1)}, u32[]{:S(2)}, u32[]{:S(2)}) %collective-permute-start.1) | collective-permute-done | bytes 524320 | tf_op jit(solution)/shard_map/ppermute | solution.py:13
  40.4 2.0 collective-permute-start.2
  42.6 10.0 %collective-permute-done.2 = f32[2,64,1024]{2,1,0:T(8,128)S(1)} collective-permute-done((f32[2,64,1024]{2,1,0:T(8,128)S(1)}, f32[2,64,1024]{2,1,0:T(8,128)S(1)}, u32[]{:S(2)}, u32[]{:S(2)}) %collective-permute-start.2) | collective-permute-done | bytes 524320 | tf_op jit(solution)/shard_map/ppermute | solution.py:13
  65.9 12.1 %collective-permute-done.5 = f32[2,64,1024]{2,1,0:T(8,128)S(1)} collective-permute-done((f32[2,64,1024]{2,1,0:T(8,128)S(1)}, f32[2,64,1024]{2,1,0:T(8,128)S(1)}, u32[]{:S(2)}, u32[]{:S(2)}) %collective-permute-start.5) | collective-permute-done | bytes 524320 | tf_op jit(solution)/shard_map/ppermute | solution.py:13
  79.3 12.4 %collective-permute-done.6 = f32[2,64,1024]{2,1,0:T(8,128)S(1)} collective-permute-done((f32[2,64,1024]{2,1,0:T(8,128)S(1)}, f32[2,64,1024]{2,1,0:T(8,128)S(1)}, u32[]{:S(2)}, u32[]{:S(2)}) %collective-permute-start.6) | collective-permute-done | bytes 524320 | tf_op jit(solution)/shard_map/ppermute | solution.py:13
  92.0 2.2 collective-permute-start.7
  97.0 8.9 %collective-permute-done.7 = f32[2,64,1024]{2,1,0:T(8,128)S(1)} collective-permute-done((f32[2,64,1024]{2,1,0:T(8,128)S(1)}, f32[2,64,1024]{2,1,0:T(8,128)S(1)}, u32[]{:S(2)}, u32[]{:S(2)}) %collective-permute-start.7) | collective-permute-done | bytes 524320 | tf_op jit(solution)/shard_map/ppermute | solution.py:13
  113.2 167.5 %all-reduce.4.cloned.1.call-done = f32[64,1024]{1,0:T(8,128)} async-done(((f32[64,1024]{1,0:T(8,128)}), f32[64,1024]{1,0:T(8,128)}) %all-reduce.4.cloned.1.call-update) | async-done | bytes 262160 | tf_op jit(solution)/shard_map/psum | solution.py:179
  283.6 4.5 collective-permute-start.9
  290.2 20.0 %fusion.37 = f32[64,1054]{1,0:T(8,128)S(1)} fusion(f32[94,1054]{1,0:T(8,128)S(1)} %select_maximum_fusion.2, f32[]{:T(128)} %bitcast.49, f32[]{:T(128)} %bitcast.48, f32[]{:T(128)} %bitcast.47, f32[]{:T(128)} %bitcast.46, f32[]{:T(128)} %bitcast.45, f32[]{:T(128)} %bitcast.44, f32[]{:T(128)} %bitcast.43, f32[]{:T(128)} %bitcast.42, f32[]{:T(128)} %bitcast.41, ...), kind=kLoop, calls=%fused_computation.122 | loop fusion | flops 4114816 | bytes 8634492 | tf_op jit(solution)/shard_map/add | solution.py:162
  310.3 21.3 %subtract_multiply_fusion = (f32[64,1024]{1,0:T(8,128)S(1)}, f32[64,1024]{1,0:T(8,128)S(1)}) fusion(s32[64,1024]{1,0:T(8,128)S(1)} %copy-done.3, f32[64,1054]{1,0:T(8,128)S(1)} %fusion.37, f32[]{:T(128)} %bitcast.2, f32[]{:T(128)} %bitcast.49, f32[]{:T(128)} %bitcast.48, f32[]{:T(128)} %bitcast.47, f32[]{:T(128)} %bitcast.46, f32[]{:T(128)} %bitcast.45, ...), kind=kLoop, calls=%fused_computation.373 | loop fusion | flops 4718592 | bytes 8913020 | tf_op jit(solution)/shard_map/mul | solution.py:184
  333.5 4.8 collective-permute-start.11
  340.2 20.0 %fusion.7 = f32[64,1054]{1,0:T(8,128)S(1)} fusion(f32[94,1054]{1,0:T(8,128)S(1)} %select_maximum_fusion, f32[]{:T(128)} %bitcast.49, f32[]{:T(128)} %bitcast.48, f32[]{:T(128)} %bitcast.47, f32[]{:T(128)} %bitcast.46, f32[]{:T(128)} %bitcast.45, f32[]{:T(128)} %bitcast.44, f32[]{:T(128)} %bitcast.43, f32[]{:T(128)} %bitcast.42, f32[]{:T(128)} %bitcast.41, ...), kind=kLoop, calls=%fused_computation.61 | loop fusion | flops 4114816 | bytes 8634492 | tf_op jit(solution)/shard_map/add | solution.py:162
  360.2 21.3 %fusion.70 = (f32[8,8,8,128]{3,1,2,0:T(8,128)S(1)}, f32[64,1024]{1,0:T(8,128)S(1)}) fusion(f32[8,8,8,128]{3,2,1,0:T(8,128)S(1)} %bitcast.291, f32[64,1054]{1,0:T(8,128)S(1)} %fusion.7, f32[]{:T(128)} %bitcast.3, f32[]{:T(128)} %bitcast.21, f32[]{:T(128)} %bitcast.22, f32[]{:T(128)} %bitcast.23, f32[]{:T(128)} %bitcast.24, f32[]{:T(128)} %bitcast.25, ...), kind=kLoop, calls=%fused_computation.189 | loop fusion | flops 4128768 | bytes 8913024
  386.0 2.2 collective-permute-start.12
  388.2 13.8 %collective-permute-done.12 = f32[2,64,1024]{2,1,0:T(8,128)S(1)} collective-permute-done((f32[2,64,1024]{2,1,0:T(8,128)S(1)}, f32[2,64,1024]{2,1,0:T(8,128)S(1)}, u32[]{:S(2)}, u32[]{:S(2)}) %collective-permute-start.12) | collective-permute-done | bytes 524320 | tf_op jit(solution)/shard_map/ppermute | solution.py:13
  402.6 13.2 %collective-permute-done.13 = f32[2,64,1024]{2,1,0:T(8,128)S(1)} collective-permute-done((f32[2,64,1024]{2,1,0:T(8,128)S(1)}, f32[2,64,1024]{2,1,0:T(8,128)S(1)}, u32[]{:S(2)}, u32[]{:S(2)}) %collective-permute-start.13) | collective-permute-done | bytes 524320 | tf_op jit(solution)/shard_map/ppermute | solution.py:13
  416.2 12.7 %collective-permute-done.14 = f32[2,64,1024]{2,1,0:T(8,128)S(1)} collective-permute-done((f32[2,64,1024]{2,1,0:T(8,128)S(1)}, f32[2,64,1024]{2,1,0:T(8,128)S(1)}, u32[]{:S(2)}, u32[]{:S(2)}) %collective-permute-start.14) | collective-permute-done | bytes 524320 | tf_op jit(solution)/shard_map/ppermute | solution.py:13
  439.6 12.6 %collective-permute-done.17 = f32[2,64,1024]{2,1,0:T(8,128)S(1)} collective-permute-done((f32[2,64,1024]{2,1,0:T(8,128)S(1)}, f32[2,64,1024]{2,1,0:T(8,128)S(1)}, u32[]{:S(2)}, u32[]{:S(2)}) %collective-permute-start.17) | collective-permute-done | bytes 524320 | tf_op jit(solution)/shard_map/ppermute | solution.py:13
  454.0 11.9 %collective-permute-done.18 = f32[2,64,1024]{2,1,0:T(8,128)S(1)} collective-permute-done((f32[2,64,1024]{2,1,0:T(8,128)S(1)}, f32[2,64,1024]{2,1,0:T(8,128)S(1)}, u32[]{:S(2)}, u32[]{:S(2)}) %collective-permute-start.18) | collective-permute-done | bytes 524320 | tf_op jit(solution)/shard_map/ppermute | solution.py:13
  466.9 13.2 %collective-permute-done.19 = f32[2,64,1024]{2,1,0:T(8,128)S(1)} collective-permute-done((f32[2,64,1024]{2,1,0:T(8,128)S(1)}, f32[2,64,1024]{2,1,0:T(8,128)S(1)}, u32[]{:S(2)}, u32[]{:S(2)}) %collective-permute-start.19) | collective-permute-done | bytes 524320 | tf_op jit(solution)/shard_map/ppermute | solution.py:13
  485.6 84.6 %reduce-scatter.4.cloned.1.call-done = f32[64,64]{1,0:T(8,128)} async-done(((f32[1024,64]{1,0:T(8,128)}), f32[64,64]{1,0:T(8,128)}) %reduce-scatter.4.cloned.1.call-update) | async-done | bytes 16400
  (170 shorter events, 63.0 us)
Async XLA Ops:
  7.2 273.5 %all-reduce.4.cloned.1.call-start = ((), (), s32[]{:S(2)}) async-start(), calls=%async_computation.1 | async-start | bytes 524288 | tf_op jit(solution)/shard_map/psum | solution.py:179
  11.7 15.3 %collective-permute-start = (f32[2,64,1024]{2,1,0:T(8,128)S(1)}, f32[2,64,1024]{2,1,0:T(8,128)S(1)}, u32[]{:S(2)}, u32[]{:S(2)}) collective-permute-start(f32[2,64,1024]{2,1,0:T(8,128)S(1)} %constant_dynamic-update-slice_fusion), channel_id=1, source_target_pairs={{0,128},{16,144},{32,160},{48,176},{64,192},{80,208},{96,224},{112... | collective-permute-start | bytes 1572872 | tf_op jit(solution)/shard_map/ppermute | solution.py:13
  27.2 12.9 %collective-permute-start.1 = (f32[2,64,1024]{2,1,0:T(8,128)S(1)}, f32[2,64,1024]{2,1,0:T(8,128)S(1)}, u32[]{:S(2)}, u32[]{:S(2)}) collective-permute-start(f32[2,64,1024]{2,1,0:T(8,128)S(1)} %maximum_select_fusion), channel_id=1, source_target_pairs={{0,64},{16,80},{32,96},{48,112},{64,0},{80,16},{96,32},{112,48},{1... | collective-permute-start | bytes 1572872 | tf_op jit(solution)/shard_map/ppermute | solution.py:13
  40.4 12.2 %collective-permute-start.2 = (f32[2,64,1024]{2,1,0:T(8,128)S(1)}, f32[2,64,1024]{2,1,0:T(8,128)S(1)}, u32[]{:S(2)}, u32[]{:S(2)}) collective-permute-start(f32[2,64,1024]{2,1,0:T(8,128)S(1)} %maximum_select_fusion.1), channel_id=1, source_target_pairs={{0,32},{16,48},{32,0},{48,16},{64,96},{80,112},{96,64},{112,80},{1... | collective-permute-start | bytes 1572872 | tf_op jit(solution)/shard_map/ppermute | solution.py:13
  52.8 3.7 collective-permute-start.3
  61.2 2.5 collective-permute-start.4
  63.9 14.1 %collective-permute-start.5 = (f32[2,64,1024]{2,1,0:T(8,128)S(1)}, f32[2,64,1024]{2,1,0:T(8,128)S(1)}, u32[]{:S(2)}, u32[]{:S(2)}) collective-permute-start(f32[2,64,1024]{2,1,0:T(8,128)S(1)} %add_select_fusion.7), channel_id=1, source_target_pairs={{0,32},{16,48},{32,0},{48,16},{64,96},{80,112},{96,64},{112,80},{1... | collective-permute-start | bytes 1572872 | tf_op jit(solution)/shard_map/ppermute | solution.py:13
  78.5 13.2 %collective-permute-start.6 = (f32[2,64,1024]{2,1,0:T(8,128)S(1)}, f32[2,64,1024]{2,1,0:T(8,128)S(1)}, u32[]{:S(2)}, u32[]{:S(2)}) collective-permute-start(f32[2,64,1024]{2,1,0:T(8,128)S(1)} %add_select_fusion.6), channel_id=1, source_target_pairs={{0,64},{16,80},{32,96},{48,112},{64,0},{80,16},{96,32},{112,48},{1... | collective-permute-start | bytes 1572872 | tf_op jit(solution)/shard_map/ppermute | solution.py:13
  92.0 13.9 %collective-permute-start.7 = (f32[2,64,1024]{2,1,0:T(8,128)S(1)}, f32[2,64,1024]{2,1,0:T(8,128)S(1)}, u32[]{:S(2)}, u32[]{:S(2)}) collective-permute-start(f32[2,64,1024]{2,1,0:T(8,128)S(1)} %add_select_fusion.5), channel_id=1, source_target_pairs={{0,128},{16,144},{32,160},{48,176},{64,192},{80,208},{96,224},{112... | collective-permute-start | bytes 1572872 | tf_op jit(solution)/shard_map/ppermute | solution.py:13
  111.9 458.3 %reduce-scatter.4.cloned.1.call-start = ((), (), s32[]{:S(2)}) async-start(), calls=%async_computation.2 | async-start | bytes 557056
  280.7 9.3 %copy-start = (f32[64,1024]{1,0:T(8,128)S(1)}, f32[64,1024]{1,0:T(8,128)}, u32[]{:S(2)}) copy-start(f32[64,1024]{1,0:T(8,128)} %all-reduce.4.cloned.1.call-done) | copy-start | bytes 786436
  281.6 7.2 %collective-permute-start.8 = (f32[15,1024]{1,0:T(8,128)S(1)}, f32[15,1024]{1,0:T(8,128)S(1)}, u32[]{:S(2)}, u32[]{:S(2)}) collective-permute-start(f32[15,1024]{1,0:T(8,128)S(1)} %get-tuple-element.54), channel_id=1, source_target_pairs={{0,16},{16,32},{32,48},{48,64},{64,80},{80,96},{96,112},{112,128},... | collective-permute-start | bytes 184328 | tf_op jit(solution)/shard_map/ppermute | solution.py:23
  283.6 6.4 %collective-permute-start.9 = (f32[15,1024]{1,0:T(8,128)S(1)}, f32[15,1024]{1,0:T(8,128)S(1)}, u32[]{:S(2)}, u32[]{:S(2)}) collective-permute-start(f32[15,1024]{1,0:T(8,128)S(1)} %get-tuple-element.55), channel_id=1, source_target_pairs={{16,0},{32,16},{48,32},{64,48},{80,64},{96,80},{112,96},{128,112},... | collective-permute-start | bytes 184328 | tf_op jit(solution)/shard_map/ppermute | solution.py:24
  290.2 20.1 %copy-start.3 = (s32[64,1024]{1,0:T(8,128)S(1)}, s32[64,1024]{1,0:T(8,128)}, u32[]{:S(2)}) copy-start(s32[64,1024]{1,0:T(8,128)} %param.11) | copy-start | bytes 786436
  331.6 7.4 %collective-permute-start.10 = (f32[15,1024]{1,0:T(8,128)S(1)}, f32[15,1024]{1,0:T(8,128)S(1)}, u32[]{:S(2)}, u32[]{:S(2)}) collective-permute-start(f32[15,1024]{1,0:T(8,128)S(1)} %get-tuple-element.52), channel_id=1, source_target_pairs={{0,16},{16,32},{32,48},{48,64},{64,80},{80,96},{96,112},{112,128},... | collective-permute-start | bytes 184328 | tf_op jit(solution)/shard_map/ppermute | solution.py:23
  333.5 6.5 %collective-permute-start.11 = (f32[15,1024]{1,0:T(8,128)S(1)}, f32[15,1024]{1,0:T(8,128)S(1)}, u32[]{:S(2)}, u32[]{:S(2)}) collective-permute-start(f32[15,1024]{1,0:T(8,128)S(1)} %get-tuple-element.53), channel_id=1, source_target_pairs={{16,0},{32,16},{48,32},{64,48},{80,64},{96,80},{112,96},{128,112},... | collective-permute-start | bytes 184328 | tf_op jit(solution)/shard_map/ppermute | solution.py:24
  386.0 16.0 %collective-permute-start.12 = (f32[2,64,1024]{2,1,0:T(8,128)S(1)}, f32[2,64,1024]{2,1,0:T(8,128)S(1)}, u32[]{:S(2)}, u32[]{:S(2)}) collective-permute-start(f32[2,64,1024]{2,1,0:T(8,128)S(1)} %constant_dynamic-update-slice_fusion.2), channel_id=1, source_target_pairs={{0,128},{16,144},{32,160},{48,176},{64,192},{80,208},{96,224},{112... | collective-permute-start | bytes 1572872 | tf_op jit(solution)/shard_map/ppermute | solution.py:13
  402.2 13.6 %collective-permute-start.13 = (f32[2,64,1024]{2,1,0:T(8,128)S(1)}, f32[2,64,1024]{2,1,0:T(8,128)S(1)}, u32[]{:S(2)}, u32[]{:S(2)}) collective-permute-start(f32[2,64,1024]{2,1,0:T(8,128)S(1)} %maximum_select_fusion.4), channel_id=1, source_target_pairs={{0,64},{16,80},{32,96},{48,112},{64,0},{80,16},{96,32},{112,48},{1... | collective-permute-start | bytes 1572872 | tf_op jit(solution)/shard_map/ppermute | solution.py:13
  416.1 12.8 %collective-permute-start.14 = (f32[2,64,1024]{2,1,0:T(8,128)S(1)}, f32[2,64,1024]{2,1,0:T(8,128)S(1)}, u32[]{:S(2)}, u32[]{:S(2)}) collective-permute-start(f32[2,64,1024]{2,1,0:T(8,128)S(1)} %maximum_select_fusion.5), channel_id=1, source_target_pairs={{0,32},{16,48},{32,0},{48,16},{64,96},{80,112},{96,64},{112,80},{1... | collective-permute-start | bytes 1572872 | tf_op jit(solution)/shard_map/ppermute | solution.py:13
  429.1 2.2 collective-permute-start.15
  435.9 2.0 collective-permute-start.16
  438.2 14.1 %collective-permute-start.17 = (f32[2,64,1024]{2,1,0:T(8,128)S(1)}, f32[2,64,1024]{2,1,0:T(8,128)S(1)}, u32[]{:S(2)}, u32[]{:S(2)}) collective-permute-start(f32[2,64,1024]{2,1,0:T(8,128)S(1)} %add_select_fusion.3), channel_id=1, source_target_pairs={{0,32},{16,48},{32,0},{48,16},{64,96},{80,112},{96,64},{112,80},{1... | collective-permute-start | bytes 1572872 | tf_op jit(solution)/shard_map/ppermute | solution.py:13
  452.8 13.2 %collective-permute-start.18 = (f32[2,64,1024]{2,1,0:T(8,128)S(1)}, f32[2,64,1024]{2,1,0:T(8,128)S(1)}, u32[]{:S(2)}, u32[]{:S(2)}) collective-permute-start(f32[2,64,1024]{2,1,0:T(8,128)S(1)} %add_select_fusion.2), channel_id=1, source_target_pairs={{0,64},{16,80},{32,96},{48,112},{64,0},{80,16},{96,32},{112,48},{1... | collective-permute-start | bytes 1572872 | tf_op jit(solution)/shard_map/ppermute | solution.py:13
  466.2 13.8 %collective-permute-start.19 = (f32[2,64,1024]{2,1,0:T(8,128)S(1)}, f32[2,64,1024]{2,1,0:T(8,128)S(1)}, u32[]{:S(2)}, u32[]{:S(2)}) collective-permute-start(f32[2,64,1024]{2,1,0:T(8,128)S(1)} %add_select_fusion.1), channel_id=1, source_target_pairs={{0,128},{16,144},{32,160},{48,176},{64,192},{80,208},{96,224},{112... | collective-permute-start | bytes 1572872 | tf_op jit(solution)/shard_map/ppermute | solution.py:13
  (4 other events, 3.0 us)
Sparse Core Ops, SparseCore 0:
  112.0 168.6 all-reduce.3
  485.0 85.1 reduce-scatter.3
where the time goes:
time: 588 us; the launch traced here: 579 us
  waiting for transfers between devices  406 us (69%)
  other arithmetic  90.9 us (15%)
  starting transfers between devices  29.8 us (5%)
  matrix products  23.2 us (4%)
  between operations  17 us (3%)
  local copies, waits for them, and re-layouts  11.9 us (2%)
    psum x1, waiting for transfers between devices, resist_section(): summed = lax.psum(intensity_term, 'kern')  168 us
    ppermute x16, waiting for transfers between devices, swapped(): lax.ppermute(shard, axis, [(i, i ^ 1 << apart) for i in range(lax.axis_si...  152 us
    unnamed x3, waiting for transfers between devices  84.6 us
    add x2, other arithmetic, smooth(): row_part + kernel_taps[tap_idx] * padded[tap_idx:tap_idx + extent, :]  40 us
    dot_general x42, matrix products, single(): return jnp.einsum(pattern, first_op, second_op, precision=highest)  22.4 us
    unnamed x2, other arithmetic  21.4 us
    mul x1, other arithmetic, resist_section(): slope_grad = 2.0 * (resist - goal_cells) * STEEP * resist * (1.0 - resist)  21.3 us
    ppermute x16, starting transfers between devices, swapped(): lax.ppermute(shard, axis, [(i, i ^ 1 << apart) for i in range(lax.axis_si...  16.5 us
  transfers between devices with their start and end apart: 22, of which 19 were waited for; matrix products, arithmetic and copies ran while one was open for 1% of the time, Pallas kernels for 0%

commit v1 on v0

--- a/solution.py
+++ b/solution.py
@@ -176,7 +176,7 @@
         padded = padded_2(values, (("slab", 0),), reach)
         return jnp.pad(padded, ((0, 0), (reach, reach)))
 
-    summed = lax.psum(intensity_term, "kern")
+    summed = jnp.sum(lax.all_gather(intensity_term, "kern"), axis=0)
     goal_cells = target.astype(jnp.float32)
     resist = jax.nn.sigmoid(
         STEEP * (smooth(widen(summed), kernel_taps, extent, full_width) - LEVEL)

time: 588 us -> 502 us (0.85)
  waiting for transfers between devices: 406 us -> 315 us
    psum x1 -> x0, waiting for transfers between devices: 168 us -> none  [resist_section(): summed = lax.psum(intensity_term, 'kern')]
    all_gather x0 -> x1, waiting for transfers between devices: none -> 77.1 us  [resist_section(): summed = jnp.sum(lax.all_gather(intensity_term, 'kern'), axis=0)]
where the time goes in v1:
time: 502 us; the launch traced here: 492 us
  waiting for transfers between devices  315 us (63%)
  other arithmetic  93.2 us (19%)
  starting transfers between devices  33.6 us (7%)
  matrix products  23.2 us (5%)
  between operations  17.1 us (3%)
  local copies, waits for them, and re-layouts  9.74 us (2%)
    ppermute x16, waiting for transfers between devices, swapped(): lax.ppermute(shard, axis, [(i, i ^ 1 << apart) for i in range(lax.axis_si...  151 us
    unnamed x3, waiting for transfers between devices  85.5 us
    all_gather x1, waiting for transfers between devices, resist_section(): summed = jnp.sum(lax.all_gather(intensity_term, 'kern'), axis=0)  77.1 us
    add x2, other arithmetic, smooth(): row_part + kernel_taps[tap_idx] * padded[tap_idx:tap_idx + extent, :]  40.3 us
    dot_general x42, matrix products, single(): return jnp.einsum(pattern, first_op, second_op, precision=highest)  22.4 us
    unnamed x2, other arithmetic  21.5 us
    mul x1, other arithmetic, resist_section(): slope_grad = 2.0 * (resist - goal_cells) * STEEP * resist * (1.0 - resist)  21.5 us
    ppermute x16, starting transfers between devices, swapped(): lax.ppermute(shard, axis, [(i, i ^ 1 << apart) for i in range(lax.axis_si...  20.2 us
  transfers between devices with their start and end apart: 22, of which 19 were waited for; matrix products, arithmetic and copies ran while one was open for 1% of the time, Pallas kernels for 0%

profile of v1, /device:TPU:2, one launch (start us, length us, event | category | flops | bytes accessed | tf_op | source)
XLA Modules:
  0.0 492.3 jit_solution(7041798640544459344)
XLA Ops:
  14.1 12.9 %collective-permute-done = f32[2,64,1024]{2,1,0:T(8,128)S(1)} collective-permute-done((f32[2,64,1024]{2,1,0:T(8,128)S(1)}, f32[2,64,1024]{2,1,0:T(8,128)S(1)}, u32[]{:S(2)}, u32[]{:S(2)}) %collective-permute-start) | collective-permute-done | bytes 524320 | tf_op jit(solution)/shard_map/ppermute | solution.py:13
  27.8 12.3 %collective-permute-done.1 = f32[2,64,1024]{2,1,0:T(8,128)S(1)} collective-permute-done((f32[2,64,1024]{2,1,0:T(8,128)S(1)}, f32[2,64,1024]{2,1,0:T(8,128)S(1)}, u32[]{:S(2)}, u32[]{:S(2)}) %collective-permute-start.1) | collective-permute-done | bytes 524320 | tf_op jit(solution)/shard_map/ppermute | solution.py:13
  42.6 10.0 %collective-permute-done.2 = f32[2,64,1024]{2,1,0:T(8,128)S(1)} collective-permute-done((f32[2,64,1024]{2,1,0:T(8,128)S(1)}, f32[2,64,1024]{2,1,0:T(8,128)S(1)}, u32[]{:S(2)}, u32[]{:S(2)}) %collective-permute-start.2) | collective-permute-done | bytes 524320 | tf_op jit(solution)/shard_map/ppermute | solution.py:13
  65.2 12.3 %collective-permute-done.5 = f32[2,64,1024]{2,1,0:T(8,128)S(1)} collective-permute-done((f32[2,64,1024]{2,1,0:T(8,128)S(1)}, f32[2,64,1024]{2,1,0:T(8,128)S(1)}, u32[]{:S(2)}, u32[]{:S(2)}) %collective-permute-start.5) | collective-permute-done | bytes 524320 | tf_op jit(solution)/shard_map/ppermute | solution.py:13
  78.9 12.6 %collective-permute-done.6 = f32[2,64,1024]{2,1,0:T(8,128)S(1)} collective-permute-done((f32[2,64,1024]{2,1,0:T(8,128)S(1)}, f32[2,64,1024]{2,1,0:T(8,128)S(1)}, u32[]{:S(2)}, u32[]{:S(2)}) %collective-permute-start.6) | collective-permute-done | bytes 524320 | tf_op jit(solution)/shard_map/ppermute | solution.py:13
  96.1 9.8 %collective-permute-done.7 = f32[2,64,1024]{2,1,0:T(8,128)S(1)} collective-permute-done((f32[2,64,1024]{2,1,0:T(8,128)S(1)}, f32[2,64,1024]{2,1,0:T(8,128)S(1)}, u32[]{:S(2)}, u32[]{:S(2)}) %collective-permute-start.7) | collective-permute-done | bytes 524320 | tf_op jit(solution)/shard_map/ppermute | solution.py:13
  112.7 77.1 %all-gather.2.cloned.1.call-done = f32[16,64,1024]{2,1,0:T(8,128)} async-done(((f32[1,64,1024]{2,1,0:T(8,128)}), f32[16,64,1024]{2,1,0:T(8,128)}) %all-gather.2.cloned.1.call-update) | async-done | bytes 4194320 | tf_op jit(solution)/shard_map/all_gather | solution.py:179
  189.8 2.5 reduce_sum.29
  194.3 4.7 collective-permute-start.9
  201.1 20.2 %fusion.37 = f32[64,1054]{1,0:T(8,128)S(1)} fusion(f32[94,1054]{1,0:T(8,128)S(1)} %select_maximum_fusion.2, f32[]{:T(128)} %bitcast.48, f32[]{:T(128)} %bitcast.47, f32[]{:T(128)} %bitcast.46, f32[]{:T(128)} %bitcast.45, f32[]{:T(128)} %bitcast.44, f32[]{:T(128)} %bitcast.43, f32[]{:T(128)} %bitcast.42, f32[]{:T(128)} %bitcast.41, f32[]{:T(128)} %bitcast.40, ...), kind=kLoop, calls=%fused_computation.122 | loop fusion | flops 4114816 | bytes 8634492 | tf_op jit(solution)/shard_map/add | solution.py:162
  221.3 21.5 %subtract_multiply_fusion = (f32[64,1024]{1,0:T(8,128)S(1)}, f32[64,1024]{1,0:T(8,128)S(1)}) fusion(s32[64,1024]{1,0:T(8,128)S(1)} %copy-done.2, f32[64,1054]{1,0:T(8,128)S(1)} %fusion.37, f32[]{:T(128)} %bitcast.2, f32[]{:T(128)} %bitcast.48, f32[]{:T(128)} %bitcast.47, f32[]{:T(128)} %bitcast.46, f32[]{:T(128)} %bitcast.45, f32[]{:T(128)} %bitcast.44, ...), kind=kLoop, calls=%fused_computation.370 | loop fusion | flops 4718592 | bytes 8913020 | tf_op jit(solution)/shard_map/mul | solution.py:184
  242.8 4.4 collective-permute-start.10
  247.2 2.2 collective-permute-start.11
  251.4 20.1 %fusion.7 = f32[64,1054]{1,0:T(8,128)S(1)} fusion(f32[94,1054]{1,0:T(8,128)S(1)} %select_maximum_fusion, f32[]{:T(128)} %bitcast.48, f32[]{:T(128)} %bitcast.47, f32[]{:T(128)} %bitcast.46, f32[]{:T(128)} %bitcast.45, f32[]{:T(128)} %bitcast.44, f32[]{:T(128)} %bitcast.43, f32[]{:T(128)} %bitcast.42, f32[]{:T(128)} %bitcast.41, f32[]{:T(128)} %bitcast.40, ...), kind=kLoop, calls=%fused_computation.61 | loop fusion | flops 4114816 | bytes 8634492 | tf_op jit(solution)/shard_map/add | solution.py:162
  271.5 21.4 %fusion.68 = (f32[8,8,8,128]{3,1,2,0:T(8,128)S(1)}, f32[64,1024]{1,0:T(8,128)S(1)}) fusion(f32[8,8,8,128]{3,2,1,0:T(8,128)S(1)} %bitcast.283, f32[64,1054]{1,0:T(8,128)S(1)} %fusion.7, f32[]{:T(128)} %bitcast.3, f32[]{:T(128)} %bitcast.20, f32[]{:T(128)} %bitcast.21, f32[]{:T(128)} %bitcast.22, f32[]{:T(128)} %bitcast.23, f32[]{:T(128)} %bitcast.24, ...), kind=kLoop, calls=%fused_computation.185 | loop fusion | flops 4128768 | bytes 8913024
  297.4 2.7 collective-permute-start.12
  300.1 13.0 %collective-permute-done.12 = f32[2,64,1024]{2,1,0:T(8,128)S(1)} collective-permute-done((f32[2,64,1024]{2,1,0:T(8,128)S(1)}, f32[2,64,1024]{2,1,0:T(8,128)S(1)}, u32[]{:S(2)}, u32[]{:S(2)}) %collective-permute-start.12) | collective-permute-done | bytes 524320 | tf_op jit(solution)/shard_map/ppermute | solution.py:13
  313.7 14.1 %collective-permute-done.13 = f32[2,64,1024]{2,1,0:T(8,128)S(1)} collective-permute-done((f32[2,64,1024]{2,1,0:T(8,128)S(1)}, f32[2,64,1024]{2,1,0:T(8,128)S(1)}, u32[]{:S(2)}, u32[]{:S(2)}) %collective-permute-start.13) | collective-permute-done | bytes 524320 | tf_op jit(solution)/shard_map/ppermute | solution.py:13
  329.6 12.0 %collective-permute-done.14 = f32[2,64,1024]{2,1,0:T(8,128)S(1)} collective-permute-done((f32[2,64,1024]{2,1,0:T(8,128)S(1)}, f32[2,64,1024]{2,1,0:T(8,128)S(1)}, u32[]{:S(2)}, u32[]{:S(2)}) %collective-permute-start.14) | collective-permute-done | bytes 524320 | tf_op jit(solution)/shard_map/ppermute | solution.py:13
  352.7 12.3 %collective-permute-done.17 = f32[2,64,1024]{2,1,0:T(8,128)S(1)} collective-permute-done((f32[2,64,1024]{2,1,0:T(8,128)S(1)}, f32[2,64,1024]{2,1,0:T(8,128)S(1)}, u32[]{:S(2)}, u32[]{:S(2)}) %collective-permute-start.17) | collective-permute-done | bytes 524320 | tf_op jit(solution)/shard_map/ppermute | solution.py:13
  366.0 12.7 %collective-permute-done.18 = f32[2,64,1024]{2,1,0:T(8,128)S(1)} collective-permute-done((f32[2,64,1024]{2,1,0:T(8,128)S(1)}, f32[2,64,1024]{2,1,0:T(8,128)S(1)}, u32[]{:S(2)}, u32[]{:S(2)}) %collective-permute-start.18) | collective-permute-done | bytes 524320 | tf_op jit(solution)/shard_map/ppermute | solution.py:13
  379.0 2.5 collective-permute-start.19
  381.5 11.4 %collective-permute-done.19 = f32[2,64,1024]{2,1,0:T(8,128)S(1)} collective-permute-done((f32[2,64,1024]{2,1,0:T(8,128)S(1)}, f32[2,64,1024]{2,1,0:T(8,128)S(1)}, u32[]{:S(2)}, u32[]{:S(2)}) %collective-permute-start.19) | collective-permute-done | bytes 524320 | tf_op jit(solution)/shard_map/ppermute | solution.py:13
  398.3 85.5 %reduce-scatter.4.cloned.1.call-done = f32[64,64]{1,0:T(8,128)} async-done(((f32[1024,64]{1,0:T(8,128)}), f32[64,64]{1,0:T(8,128)}) %reduce-scatter.4.cloned.1.call-update) | async-done | bytes 16400
  (170 shorter events, 65.0 us)
Async XLA Ops:
  7.2 182.7 %all-gather.2.cloned.1.call-start = ((), (), s32[]{:S(2)}) async-start(), calls=%async_computation.1 | async-start | bytes 4456448 | tf_op jit(solution)/shard_map/all_gather | solution.py:179
  11.7 15.3 %collective-permute-start = (f32[2,64,1024]{2,1,0:T(8,128)S(1)}, f32[2,64,1024]{2,1,0:T(8,128)S(1)}, u32[]{:S(2)}, u32[]{:S(2)}) collective-permute-start(f32[2,64,1024]{2,1,0:T(8,128)S(1)} %constant_dynamic-update-slice_fusion), channel_id=1, source_target_pairs={{0,128},{16,144},{32,160},{48,176},{64,192},{80,208},{96,224},{112... | collective-permute-start | bytes 1572872 | tf_op jit(solution)/shard_map/ppermute | solution.py:13
  27.2 12.9 %collective-permute-start.1 = (f32[2,64,1024]{2,1,0:T(8,128)S(1)}, f32[2,64,1024]{2,1,0:T(8,128)S(1)}, u32[]{:S(2)}, u32[]{:S(2)}) collective-permute-start(f32[2,64,1024]{2,1,0:T(8,128)S(1)} %maximum_select_fusion), channel_id=1, source_target_pairs={{0,64},{16,80},{32,96},{48,112},{64,0},{80,16},{96,32},{112,48},{1... | collective-permute-start | bytes 1572872 | tf_op jit(solution)/shard_map/ppermute | solution.py:13
  40.4 12.2 %collective-permute-start.2 = (f32[2,64,1024]{2,1,0:T(8,128)S(1)}, f32[2,64,1024]{2,1,0:T(8,128)S(1)}, u32[]{:S(2)}, u32[]{:S(2)}) collective-permute-start(f32[2,64,1024]{2,1,0:T(8,128)S(1)} %maximum_select_fusion.1), channel_id=1, source_target_pairs={{0,32},{16,48},{32,0},{48,16},{64,96},{80,112},{96,64},{112,80},{1... | collective-permute-start | bytes 1572872 | tf_op jit(solution)/shard_map/ppermute | solution.py:13
  52.8 2.9 collective-permute-start.3
  60.4 2.6 collective-permute-start.4
  63.2 14.3 %collective-permute-start.5 = (f32[2,64,1024]{2,1,0:T(8,128)S(1)}, f32[2,64,1024]{2,1,0:T(8,128)S(1)}, u32[]{:S(2)}, u32[]{:S(2)}) collective-permute-start(f32[2,64,1024]{2,1,0:T(8,128)S(1)} %add_select_fusion.7), channel_id=1, source_target_pairs={{0,32},{16,48},{32,0},{48,16},{64,96},{80,112},{96,64},{112,80},{1... | collective-permute-start | bytes 1572872 | tf_op jit(solution)/shard_map/ppermute | solution.py:13
  77.8 17.0 %copy-start.4 = (f32[16]{0:T(128)S(1)}, f32[16]{0:T(128)}, u32[]{:S(2)}) copy-start(f32[16]{0:T(128)} %param.8) | copy-start | bytes 196
  78.1 13.4 %collective-permute-start.6 = (f32[2,64,1024]{2,1,0:T(8,128)S(1)}, f32[2,64,1024]{2,1,0:T(8,128)S(1)}, u32[]{:S(2)}, u32[]{:S(2)}) collective-permute-start(f32[2,64,1024]{2,1,0:T(8,128)S(1)} %add_select_fusion.6), channel_id=1, source_target_pairs={{0,64},{16,80},{32,96},{48,112},{64,0},{80,16},{96,32},{112,48},{1... | collective-permute-start | bytes 1572872 | tf_op jit(solution)/shard_map/ppermute | solution.py:13
  91.8 14.1 %collective-permute-start.7 = (f32[2,64,1024]{2,1,0:T(8,128)S(1)}, f32[2,64,1024]{2,1,0:T(8,128)S(1)}, u32[]{:S(2)}, u32[]{:S(2)}) collective-permute-start(f32[2,64,1024]{2,1,0:T(8,128)S(1)} %add_select_fusion.5), channel_id=1, source_target_pairs={{0,128},{16,144},{32,160},{48,176},{64,192},{80,208},{96,224},{112... | collective-permute-start | bytes 1572872 | tf_op jit(solution)/shard_map/ppermute | solution.py:13
  111.9 371.9 %reduce-scatter.4.cloned.1.call-start = ((), (), s32[]{:S(2)}) async-start(), calls=%async_computation.2 | async-start | bytes 557056
  192.3 7.4 %collective-permute-start.8 = (f32[15,1024]{1,0:T(8,128)S(1)}, f32[15,1024]{1,0:T(8,128)S(1)}, u32[]{:S(2)}, u32[]{:S(2)}) collective-permute-start(f32[15,1024]{1,0:T(8,128)S(1)} %get-tuple-element.54), channel_id=1, source_target_pairs={{0,16},{16,32},{32,48},{48,64},{64,80},{80,96},{96,112},{112,128},... | collective-permute-start | bytes 184328 | tf_op jit(solution)/shard_map/ppermute | solution.py:23
  194.3 6.6 %collective-permute-start.9 = (f32[15,1024]{1,0:T(8,128)S(1)}, f32[15,1024]{1,0:T(8,128)S(1)}, u32[]{:S(2)}, u32[]{:S(2)}) collective-permute-start(f32[15,1024]{1,0:T(8,128)S(1)} %get-tuple-element.55), channel_id=1, source_target_pairs={{16,0},{32,16},{48,32},{64,48},{80,64},{96,80},{112,96},{128,112},... | collective-permute-start | bytes 184328 | tf_op jit(solution)/shard_map/ppermute | solution.py:24
  201.1 20.2 %copy-start.2 = (s32[64,1024]{1,0:T(8,128)S(1)}, s32[64,1024]{1,0:T(8,128)}, u32[]{:S(2)}) copy-start(s32[64,1024]{1,0:T(8,128)} %param.11) | copy-start | bytes 786436
  242.8 7.4 %collective-permute-start.10 = (f32[15,1024]{1,0:T(8,128)S(1)}, f32[15,1024]{1,0:T(8,128)S(1)}, u32[]{:S(2)}, u32[]{:S(2)}) collective-permute-start(f32[15,1024]{1,0:T(8,128)S(1)} %get-tuple-element.52), channel_id=1, source_target_pairs={{0,16},{16,32},{32,48},{48,64},{64,80},{80,96},{96,112},{112,128},... | collective-permute-start | bytes 184328 | tf_op jit(solution)/shard_map/ppermute | solution.py:23
  247.2 4.0 collective-permute-start.11
  297.4 15.7 %collective-permute-start.12 = (f32[2,64,1024]{2,1,0:T(8,128)S(1)}, f32[2,64,1024]{2,1,0:T(8,128)S(1)}, u32[]{:S(2)}, u32[]{:S(2)}) collective-permute-start(f32[2,64,1024]{2,1,0:T(8,128)S(1)} %constant_dynamic-update-slice_fusion.2), channel_id=1, source_target_pairs={{0,128},{16,144},{32,160},{48,176},{64,192},{80,208},{96,224},{112... | collective-permute-start | bytes 1572872 | tf_op jit(solution)/shard_map/ppermute | solution.py:13
  313.4 14.4 %collective-permute-start.13 = (f32[2,64,1024]{2,1,0:T(8,128)S(1)}, f32[2,64,1024]{2,1,0:T(8,128)S(1)}, u32[]{:S(2)}, u32[]{:S(2)}) collective-permute-start(f32[2,64,1024]{2,1,0:T(8,128)S(1)} %maximum_select_fusion.4), channel_id=1, source_target_pairs={{0,64},{16,80},{32,96},{48,112},{64,0},{80,16},{96,32},{112,48},{1... | collective-permute-start | bytes 1572872 | tf_op jit(solution)/shard_map/ppermute | solution.py:13
  328.0 13.5 %collective-permute-start.14 = (f32[2,64,1024]{2,1,0:T(8,128)S(1)}, f32[2,64,1024]{2,1,0:T(8,128)S(1)}, u32[]{:S(2)}, u32[]{:S(2)}) collective-permute-start(f32[2,64,1024]{2,1,0:T(8,128)S(1)} %maximum_select_fusion.5), channel_id=1, source_target_pairs={{0,32},{16,48},{32,0},{48,16},{64,96},{80,112},{96,64},{112,80},{1... | collective-permute-start | bytes 1572872 | tf_op jit(solution)/shard_map/ppermute | solution.py:13
  341.8 2.2 collective-permute-start.15
  348.7 2.0 collective-permute-start.16
  350.9 14.1 %collective-permute-start.17 = (f32[2,64,1024]{2,1,0:T(8,128)S(1)}, f32[2,64,1024]{2,1,0:T(8,128)S(1)}, u32[]{:S(2)}, u32[]{:S(2)}) collective-permute-start(f32[2,64,1024]{2,1,0:T(8,128)S(1)} %add_select_fusion.3), channel_id=1, source_target_pairs={{0,32},{16,48},{32,0},{48,16},{64,96},{80,112},{96,64},{112,80},{1... | collective-permute-start | bytes 1572872 | tf_op jit(solution)/shard_map/ppermute | solution.py:13
  365.5 13.2 %collective-permute-start.18 = (f32[2,64,1024]{2,1,0:T(8,128)S(1)}, f32[2,64,1024]{2,1,0:T(8,128)S(1)}, u32[]{:S(2)}, u32[]{:S(2)}) collective-permute-start(f32[2,64,1024]{2,1,0:T(8,128)S(1)} %add_select_fusion.2), channel_id=1, source_target_pairs={{0,64},{16,80},{32,96},{48,112},{64,0},{80,16},{96,32},{112,48},{1... | collective-permute-start | bytes 1572872 | tf_op jit(solution)/shard_map/ppermute | solution.py:13
  379.0 13.8 %collective-permute-start.19 = (f32[2,64,1024]{2,1,0:T(8,128)S(1)}, f32[2,64,1024]{2,1,0:T(8,128)S(1)}, u32[]{:S(2)}, u32[]{:S(2)}) collective-permute-start(f32[2,64,1024]{2,1,0:T(8,128)S(1)} %add_select_fusion.1), channel_id=1, source_target_pairs={{0,128},{16,144},{32,160},{48,176},{64,192},{80,208},{96,224},{112... | collective-permute-start | bytes 1572872 | tf_op jit(solution)/shard_map/ppermute | solution.py:13
  (3 other events, 34.9 us)
Sparse Core Ops, SparseCore 0:
  112.1 77.7 all-gather.1
  397.7 86.0 reduce-scatter.3
